TPU v7x, 32 devices: a whole 2x2x4 slice. The times are simulated.
32 devices in a mesh: ctx: 8 (over z, y), head: 4 (over x, core).
Axes of the slice: x: 2, y: 2, z: 4, core: 2. Of those that a mesh axis runs over, the one named last changes fastest.
Arguments:
- query: bfloat16 [8, 64, 576], P('ctx', 'head'), may hold values from -20 to 20
- cache: bfloat16 [32768, 576], P('ctx'), may hold values from -20 to 20
- cotangent: bfloat16 [8, 64, 512], P('ctx', 'head'), may hold values from -6 to 6
- positions: int32 [8], P('ctx'), may hold values from 0 to 262143
- visible: int32 [8], replicated, may hold values from 128 to 32768, as said below
Outputs:
- attention: bfloat16 [8, 64, 512], P('ctx', 'head')
- grad_query: float32 [8, 64, 576], P('ctx', 'head')
- grad_cache: bfloat16 [32768, 576], P('ctx')
Inputs may be any that keep to these rules, and one draw needn't show every extreme that they name: `visible`: each entry is a multiple of 128; some rollout token sees all 32768 prompt tokens.
All inputs are finite; a program needn't handle non-finite values.
Results may differ from a plain program's by a relative error of at most 0.01855.
Values may be sent and summed in bfloat16 or wider, within the bound.
No kernel may reach another device: no remote copies, remote signals or barrier semaphores. Data moves between devices by JAX's collectives and lax.ppermute only.
A program may use at most 128 MiB of HBM per device.

v0:
```python
import jax
import jax.numpy as jnp
import numpy as np
from jax import lax
from jax.sharding import PartitionSpec as P

softmax_scale = 192.0 ** (-0.5)
position_bits = 18
masked_value = -1e30


def rotation(positions, half_width):
    frequency = 10000.0 ** (-np.arange(half_width) / half_width)
    angles = np.outer(2.0 ** np.arange(position_bits), frequency)
    cosine_table = jnp.asarray(np.cos(angles), jnp.float32)
    sine_table = jnp.asarray(np.sin(angles), jnp.float32)
    cosines = jnp.ones((positions.shape[0], half_width), jnp.float32)
    sine_part = jnp.zeros((positions.shape[0], half_width), jnp.float32)
    for bit_index in range(position_bits):
        switch = (positions // 2**bit_index % 2).astype(jnp.float32)[:, None]
        step_cos = 1.0 + switch * (cosine_table[bit_index] - 1.0)
        step_sin = switch * sine_table[bit_index]
        cosines, sine_part = (
            cosines * step_cos - sine_part * step_sin,
            sine_part * step_cos + cosines * step_sin,
        )
    return (cosines[:, None, :], sine_part[:, None, :])


def rotate(tensor, cosines, sine_part, value_width, inverse):
    half_width = cosines.shape[-1]
    lower = tensor[..., value_width : value_width + half_width]
    upper = tensor[..., value_width + half_width :]
    if inverse:
        sine_part = -sine_part
    new_lower = lower * cosines - upper * sine_part
    new_upper = lower * sine_part + upper * cosines
    return jnp.concatenate([tensor[..., :value_width], new_lower, new_upper], axis=-1)


def body(query, cache, cotangent, positions, visible):
    value_width = cotangent.shape[-1]
    half_width = (query.shape[-1] - value_width) // 2
    extra_width = cache.shape[1] - value_width
    cosines, sine_part = rotation(positions, half_width)
    rotated = rotate(query.astype(jnp.float32), cosines, sine_part, value_width, False).astype(
        jnp.bfloat16
    )
    rotated, gradients = (
        lax.all_gather(rotated, "ctx", axis=0, tiled=True),
        lax.all_gather(cotangent, "ctx", axis=0, tiled=True),
    )
    block_rows = cache.shape[0]
    first_key = lax.axis_index("ctx") * block_rows
    key_index = first_key + jnp.arange(block_rows)
    allowed = key_index[None, None, :] < visible[:, None, None]
    scores = (
        jnp.einsum("thl,kl->thk", rotated, cache, preferred_element_type=jnp.float32)
        * softmax_scale
    )
    scores = jnp.where(allowed, scores, masked_value)
    local_peak = jnp.max(scores, axis=2)
    peak = lax.pmax(local_peak, "ctx")
    weights = jnp.where(allowed, jnp.exp(scores - peak[..., None]), 0.0)
    local_mass = jnp.sum(weights, axis=2)
    mass = lax.psum(local_mass, "ctx")
    probs = weights / mass[..., None]
    prob_low = probs.astype(jnp.bfloat16)
    values = cache[:, :value_width]
    attended = jnp.einsum("thk,kv->thv", prob_low, values, preferred_element_type=jnp.float32)
    attention = lax.psum_scatter(attended, "ctx", scatter_dimension=0, tiled=True).astype(
        jnp.bfloat16
    )
    grad_probs = jnp.einsum("thv,kv->thk", gradients, values, preferred_element_type=jnp.float32)
    local_delta = jnp.sum(prob_low.astype(jnp.float32) * grad_probs, axis=2)
    delta = lax.psum(local_delta, "ctx")
    grad_scores = (probs * (grad_probs - delta[..., None]) * softmax_scale).astype(jnp.bfloat16)
    grad_rotated = jnp.einsum("thk,kl->thl", grad_scores, cache, preferred_element_type=jnp.float32)
    grad_latent = jnp.einsum(
        "thk,thl->kl", grad_scores, rotated, preferred_element_type=jnp.float32
    )
    grad_value = jnp.einsum("thk,thv->kv", prob_low, gradients, preferred_element_type=jnp.float32)
    grad_latent = grad_latent + jnp.pad(grad_value, ((0, 0), (0, extra_width)))
    grad_cache = lax.psum(grad_latent, "head").astype(jnp.bfloat16)
    grad_rotated = lax.psum_scatter(grad_rotated, "ctx", scatter_dimension=0, tiled=True)
    grad_query = rotate(grad_rotated, cosines, sine_part, value_width, True)
    return (attention, grad_query, grad_cache)


def solution(mesh):
    placed = (P("ctx", "head", None), P("ctx", None), P("ctx", "head", None), P("ctx"), P())
    return jax.shard_map(
        body,
        mesh=mesh,
        in_specs=placed,
        out_specs=(P("ctx", "head", None), P("ctx", "head", None), P("ctx", None)),
        check_vma=False,
    )
```

profile of v0, /device:TPU:0, one launch (start us, length us, event | category | flops | bytes accessed | tf_op | source)
XLA Modules:
  0.0 339.2 jit_solution(13869444425280142998)
XLA Ops:
  7.2 0.0 reduce-scatter.3.cloned.1.call-start
  8.3 0.7 slice.130
  9.0 0.7 convert_element_type.83
  9.8 32.5 %all_gather.7 = bf16[8,16,512]{2,1,0:T(8,128)(2,1)S(1)} all-gather(bf16[1,16,512]{2,1,0:T(8,128)(2,1)} %param.9), channel_id=1, replica_groups=mesh['ctx'=8,'head'=4] {'ctx'}, dimensions={0}, use_global_device_ids=true | all-gather | bytes 147456 | tf_op jit(solution)/shard_map/all_gather | solution.py:51
  42.3 0.7 fusion.15
  43.0 0.7 fusion.18
  43.7 0.7 fusion.22
  44.5 0.7 fusion.26
  45.2 0.7 fusion.30
  46.0 0.7 fusion.34
  46.7 0.7 fusion.38
  47.5 0.7 fusion.42
  48.2 0.7 fusion.50
  49.0 0.7 fusion.49
  49.7 0.1 subtract_convert_fusion
  49.7 0.1 pad_maximum_fusion.1
  49.8 30.6 %all_gather.6 = bf16[8,16,576]{2,1,0:T(8,128)(2,1)S(1)} all-gather(bf16[1,16,576]{2,1,0:T(8,128)(2,1)S(1)} %pad_maximum_fusion.1), channel_id=1, replica_groups=mesh['ctx'=8,'head'=4] {'ctx'}, dimensions={0}, use_global_device_ids=true | all-gather | bytes 165888 | tf_op jit(solution)/shard_map/all_gather | solution.py:50
  80.4 0.7 broadcast_compare_fusion
  81.1 3.6 %fusion.69 = (f32[8,16]{1,0:T(8,128)S(1)}, f32[8,16,4096]{2,1,0:T(8,128)S(1)}) fusion(bf16[8,16,576]{2,1,0:T(8,128)(2,1)S(1)} %all_gather.6, bf16[4096,576]{0,1:T(8,128)(2,1)} %param.8, pred[8,4096]{1,0:T(8,128)(4,1)S(1)} %broadcast_compare_fusion), kind=kOutput, calls=%fused_computation.119 | convolution fusion | flops 605552512 | bytes 6996480 | tf_op jit(solution)/shard_map/thl,kl->thk/dot_general | solution.py:58
  84.8 21.4 %pmax.7 = f32[8,16]{1,0:T(8,128)S(1)} all-reduce(f32[8,16]{1,0:T(8,128)S(1)} %get-tuple-element.36), channel_id=1, replica_groups=mesh['ctx'=8,'head'=4] {'ctx'}, use_global_device_ids=true, to_apply=%region_1.2 | all-reduce | flops 128 | bytes 1024 | tf_op jit(solution)/shard_map/pmax | solution.py:63
  106.1 0.0 slice-start
  106.1 0.6 fusion.11
  106.7 17.1 %psum.21 = f32[8,16]{1,0:T(8,128)S(1)} all-reduce(f32[8,16]{1,0:T(8,128)S(1)} %fusion.11), channel_id=1, replica_groups=mesh['ctx'=8,'head'=4] {'ctx'}, use_global_device_ids=true, to_apply=%region_3.4 | all-reduce | flops 128 | bytes 1024 | tf_op jit(solution)/shard_map/psum | solution.py:66
  123.8 0.0 slice-start.1
  123.8 4.9 %multiply_reduce_fusion = (f32[8,16]{1,0:T(8,128)S(1)}, bf16[8,16,4096]{2,1,0:T(8,128)(2,1)S(1)}, f32[8,16,4096]{2,1,0:T(8,128)}) fusion(f32[8,16]{1,0:T(8,128)S(1)} %psum.21, f32[8,16,4096]{2,1,0:T(8,128)S(1)} %get-tuple-element.37, f32[8,16]{1,0:T(8,128)S(1)} %pmax.7, pred[8,4096]{1,0:T(8,128)(4,1)S(1)} %broadcast_compare_fusion, ...), kind=kOutput, calls=%fused_computation.14 | convolution fusion | flops 540540800 | bytes 9602560 | tf_op jit(solution)/shard_map/thv,kv->thk/dot_general | solution.py:74
  128.7 0.0 copy-start
  128.7 1.0 copy-done
  129.7 0.0 slice-done
  129.7 0.0 slice-done.1
  129.7 2.3 fusion.6
  132.0 0.0 reduce-scatter.3.cloned.1.call-update
  132.0 0.0 reduce-scatter.5.cloned.1.call-start
  132.1 19.1 %psum.22 = f32[8,16]{1,0:T(8,128)S(1)} all-reduce(f32[8,16]{1,0:T(8,128)S(1)} %get-tuple-element.7), channel_id=1, replica_groups=mesh['ctx'=8,'head'=4] {'ctx'}, use_global_device_ids=true, to_apply=%region_6.7 | all-reduce | flops 128 | bytes 1024 | tf_op jit(solution)/shard_map/psum | solution.py:76
  151.2 2.3 multiply_convert_fusion
  153.6 0.0 copy-start.1
  153.6 4.9 %fusion.1 = f32[8,16,576]{2,1,0:T(8,128)} fusion(bf16[8,16,4096]{2,1,0:T(8,128)(2,1)S(1)} %multiply_convert_fusion, bf16[4096,576]{0,1:T(8,128)(2,1)} %param.8), kind=kOutput, calls=%fused_computation.4 | convolution fusion | flops 603979776 | bytes 6062080 | tf_op jit(solution)/shard_map/thk,kl->thl/dot_general | solution.py:78
  158.5 0.0 reduce-scatter.5.cloned.1.call-update
  158.5 0.0 copy-done.1
  158.5 1.3 convolution_bitcast_fusion
  159.8 5.1 %bitcast_add_fusion = f32[4096,576]{0,1:T(8,128)} fusion(f32[4096,512]{0,1:T(8,128)S(1)} %convolution_bitcast_fusion, bf16[8,16,4096]{2,1,0:T(8,128)(2,1)S(1)} %multiply_convert_fusion, bf16[8,16,576]{2,1,0:T(8,128)(2,1)S(1)} %all_gather.6), kind=kOutput, calls=%fused_computation | convolution fusion | flops 606339072 | bytes 19021824 | tf_op jit(solution)/shard_map/thk,thl->kl/dot_general | solution.py:79
  164.9 163.8 %all-reduce.2 = bf16[4096,576]{0,1:T(8,128)(2,1)} all-reduce(f32[4096,576]{0,1:T(8,128)} %bitcast_add_fusion), channel_id=1, replica_groups=mesh['ctx'=8,'head'=4] {'head'}, use_global_device_ids=true, to_apply=%region_8.9 | all-reduce | flops 2359296 | bytes 14155776 | tf_op jit(solution)/shard_map/psum | solution.py:84
  328.7 0.0 reduce-scatter.3.cloned.1.call-done
  328.7 1.4 convert_element_type.103
  330.0 0.0 reduce-scatter.5.cloned.1.call-done
  330.0 0.8 slice.175
  330.8 0.9 multiply_subtract_fusion
  331.7 0.7 pad_maximum_fusion
  (2 shorter events, 0.0 us)
Async XLA Ops:
  7.2 321.5 %reduce-scatter.3.cloned.1.call-start = ((), (), s32[]{:S(2)}) async-start(), calls=%async_computation.2 | async-start | bytes 294912 | tf_op jit(solution)/shard_map/reduce_scatter | solution.py:71
  106.1 23.6 %slice-start = ((s8[4718592]{0:T(1024)(128)(4,1)}), s8[524288]{0:T(1024)(128)(4,1)S(1)}, s32[]{:S(2)}) async-start(s8[4718592]{0:T(1024)(128)(4,1)} %bitcast.51), calls=%async_computation.4 | async-start | bytes 1048576
  123.8 5.9 %slice-start.1 = ((s8[4718592]{0:T(1024)(128)(4,1)}), s8[4194304]{0:T(1024)(128)(4,1)S(1)}, s32[]{:S(2)}) async-start(s8[4718592]{0:T(1024)(128)(4,1)} %bitcast.51), calls=%async_computation.5 | async-start | bytes 8388608
  128.7 1.0 copy-start
  132.0 198.0 %reduce-scatter.5.cloned.1.call-start = ((), (), s32[]{:S(2)}) async-start(), calls=%async_computation.3 | async-start | bytes 368640 | tf_op jit(solution)/shard_map/reduce_scatter | solution.py:85
  153.6 4.9 %copy-start.1 = (bf16[8,16,4096]{2,1,0:T(8,128)(2,1)S(1)}, bf16[8,16,4096]{2,1,0:T(8,128)(2,1)}, u32[]{:S(2)}) copy-start(bf16[8,16,4096]{2,1,0:T(8,128)(2,1)} %copy-done) | copy-start | bytes 3145732
Sparse Core Ops, SparseCore 0:
  132.1 60.7 reduce-scatter.2
  196.2 61.2 reduce-scatter.4
where the time goes:
time: 340 us; the launch traced here: 339 us
  blocking collectives  285 us (84%)
  matrix products  22.1 us (6%)
  between operations  15.2 us (4%)
  other arithmetic  14.8 us (4%)
    psum x1, blocking collectives, body(): grad_cache = lax.psum(grad_latent, 'head').astype(jnp.bfloat16)  164 us
    all_gather x1, blocking collectives, body(): lax.all_gather(cotangent, 'ctx', axis=0, tiled=True)  32.5 us
    all_gather x1, blocking collectives, body(): lax.all_gather(rotated, 'ctx', axis=0, tiled=True)  30.6 us
    pmax x1, blocking collectives, body(): peak = lax.pmax(local_peak, 'ctx')  21.4 us
    psum x1, blocking collectives, body(): delta = lax.psum(local_delta, 'ctx')  19.1 us
    psum x1, blocking collectives, body(): mass = lax.psum(local_mass, 'ctx')  17.1 us
  transfers between devices with their start and end apart: 2, of which 0 were waited for; matrix products, arithmetic and copies ran while one was open for 4% of the time, Pallas kernels for 0%

commit v1 on v0

v1 whole, which is shorter than its diff:
```python
import functools

import jax
import jax.numpy as jnp
import numpy as np
from jax import lax
from jax.experimental import pallas as pl
from jax.experimental.pallas import tpu as pltpu
from jax.sharding import PartitionSpec as P

softmax_scale = 192.0 ** (-0.5)
exp2_scale = softmax_scale * float(np.log2(np.e))
position_bits = 18
masked_value = -1e30
peak_floor = -1e29

MINOR = (((1,), (1,)), ((), ()))
MAJOR = (((1,), (0,)), ((), ()))


def matmul(a, b, dims):
    return lax.dot_general(a, b, dims, preferred_element_type=jnp.float32)


def rotation_tables(half_width):
    frequency = 10000.0 ** (-np.arange(half_width) / half_width)
    angles = np.outer(2.0 ** np.arange(position_bits), frequency)
    cosine = np.cos(angles).astype(np.float32)
    sine = np.sin(angles).astype(np.float32)
    return np.concatenate([cosine, cosine], 1), np.concatenate([-sine, sine], 1)


def swap_matrix(half_width):
    return np.roll(np.eye(2 * half_width, dtype=np.float32), half_width, 0)


def prepare_kernel(position_ref, query_ref, cotangent_ref, cos_ref, sin_ref, swap_ref, packed_ref, turn_ref):
    tokens, heads, width = query_ref.shape
    values = cotangent_ref.shape[2]
    rotary = width - values
    swap = swap_ref[...].astype(jnp.bfloat16)
    for t in range(tokens):
        position = position_ref[t]
        cosine = jnp.ones((1, rotary), jnp.float32)
        sine = jnp.zeros((1, rotary), jnp.float32)
        for bit in range(position_bits):
            switch = (lax.shift_right_logical(position, bit) & 1).astype(jnp.float32)
            step_cos = 1.0 + switch * (cos_ref[bit : bit + 1, :] - 1.0)
            step_sin = switch * sin_ref[bit : bit + 1, :]
            cosine, sine = cosine * step_cos - sine * step_sin, sine * step_cos + cosine * step_sin
        turn_ref[t, 0:1, :] = cosine
        turn_ref[t, 1:2, :] = sine
        rope = query_ref[t, :, values:]
        turned = rope.astype(jnp.float32) * cosine + matmul(rope, swap, MAJOR) * sine
        for c in range(packed_ref.shape[0]):
            packed_ref[c, t, :, :values] = cotangent_ref[t]
            packed_ref[c, t, :, values : 2 * values] = query_ref[t, :, :values]
            packed_ref[c, t, :, 2 * values :] = turned.astype(jnp.bfloat16)


def score_kernel(chunks, heads, first_ref, visible_ref, packed_ref, cache_ref, weights_ref, stats_ref, cache_buf, scores, grads, sems):
    rows = packed_ref.shape[0]
    keys, width = cache_ref.shape
    values = packed_ref.shape[1] - width
    tokens = rows // heads
    size = keys // chunks

    def fetch(c):
        part = pl.ds(c * size, size)
        return pltpu.make_async_copy(cache_ref.at[part], cache_buf.at[part], sems.at[c])

    for c in range(chunks):
        fetch(c).start()
    token_of = lax.broadcasted_iota(jnp.int32, (rows, 1), 0) // heads
    limit = jnp.zeros((rows, 1), jnp.int32)
    for t in range(tokens):
        limit = jnp.where(token_of == t, visible_ref[t], limit)
    limit = limit - first_ref[0]
    cotangent = packed_ref[:, :values]
    rotated = packed_ref[:, values:]
    peak = jnp.full((rows, 128), peak_floor, jnp.float32)
    lane = lax.broadcasted_iota(jnp.int32, (rows, size), 1)
    for c in range(chunks):
        fetch(c).wait()
        block = cache_buf[c * size : (c + 1) * size, :]
        score = matmul(rotated, block, MINOR) * exp2_scale
        score = jnp.where(lane < limit - c * size, score, masked_value)
        scores[:, c * size : (c + 1) * size] = score
        for i in range(size // 128):
            peak = jnp.maximum(peak, score[:, i * 128 : (i + 1) * 128])
        grads[:, c * size : (c + 1) * size] = matmul(cotangent, block[:, :values], MINOR)
    peak = jnp.max(peak, axis=1, keepdims=True)
    mass = jnp.zeros((rows, 128), jnp.float32)
    moment = jnp.zeros((rows, 128), jnp.float32)
    for i in range(keys // 128):
        part = slice(i * 128, (i + 1) * 128)
        weight = jnp.exp2(scores[:, part] - peak)
        scores[:, part] = weight
        mass = mass + weight
        moment = moment + weight * grads[:, part]
    mass = jnp.sum(mass, axis=1, keepdims=True)
    moment = jnp.sum(moment, axis=1, keepdims=True)
    centre = jnp.where(mass > 0.0, moment / jnp.where(mass > 0.0, mass, 1.0), 0.0)
    for i in range(keys // size):
        part = slice(i * size, (i + 1) * size)
        weight = scores[:, part]
        low = weight.astype(jnp.bfloat16)
        lean = (weight * (grads[:, part] - centre)).astype(jnp.bfloat16)
        for t in range(tokens):
            weights_ref[t, :heads, part] = low[t * heads : (t + 1) * heads]
            weights_ref[t, heads:, part] = lean[t * heads : (t + 1) * heads]
    column = lax.broadcasted_iota(jnp.int32, (rows, 128), 1)
    table = jnp.where(column == 0, peak, jnp.where(column == 1, mass, jnp.where(column == 2, centre, 0.0)))
    table = jnp.transpose(table)[:8, :]
    for n in range(stats_ref.shape[0]):
        stats_ref[n] = table


def combine(stats):
    top = functools.reduce(jnp.maximum, [s[0] for s in stats])
    shares = [jnp.exp2(s[0] - top) for s in stats]
    mass = functools.reduce(jnp.add, [f * s[1] for f, s in zip(shares, stats)])
    moment = functools.reduce(jnp.add, [f * s[1] * s[2] for f, s in zip(shares, stats)])
    return top, shares, mass, moment / mass


def latent_kernel(heads, offsets, first_ref, head_ref, visible_ref, stats_ref, cache_ref, *refs):
    slots = refs[: len(offsets)]
    out_ref, packed, log_mass, delta_ref, limit_ref, sems = refs[len(offsets) :]
    keys, width = cache_ref.shape
    values = packed.shape[1] - width
    rows = slots[0].shape[0]
    tokens = rows // heads
    total = packed.shape[0]
    step = pl.program_id(0)

    @pl.when(step == 0)
    def _():
        copies = [
            pltpu.make_async_copy(slot, packed.at[pl.ds(j * rows, rows)], sems.at[j])
            for j, slot in enumerate(slots)
        ]
        for copy in copies:
            copy.start()
        token_of = lax.broadcasted_iota(jnp.int32, (1, rows), 1) // heads
        limit = jnp.zeros((1, rows), jnp.int32)
        for t in range(tokens):
            limit = jnp.where(token_of == t, visible_ref[t], limit)
        limit = limit - first_ref[0]
        for j, offset in enumerate(offsets):
            group = head_ref[0] ^ offset
            parts = [stats_ref[c, group] for c in range(stats_ref.shape[0])]
            top, _, mass, delta = combine([(p[0:1], p[1:2], p[2:3]) for p in parts])
            log_mass[:, j * rows : (j + 1) * rows] = top + jnp.log2(mass)
            delta_ref[:, j * rows : (j + 1) * rows] = delta
            limit_ref[:, j * rows : (j + 1) * rows] = limit
        for copy in copies:
            copy.wait()

    block = cache_ref[...]
    span = min(512, total)
    key = lax.broadcasted_iota(jnp.int32, (keys, span), 0) + step * keys
    acc = None
    for r in range(total // span):
        part = slice(r * span, (r + 1) * span)
        cotangent = packed[part, :values]
        rotated = packed[part, values:]
        score = matmul(block, rotated, MINOR) * exp2_scale
        score = jnp.where(key < limit_ref[:, part], score - log_mass[:, part], masked_value)
        prob = jnp.exp2(score)
        grad = matmul(block[:, :values], cotangent, MINOR)
        lean = (prob * (grad - delta_ref[:, part]) * softmax_scale).astype(jnp.bfloat16)
        main = matmul(lean, rotated[:, :values], MAJOR) + matmul(prob.astype(jnp.bfloat16), cotangent, MAJOR)
        side = matmul(lean, rotated[:, values:], MAJOR)
        acc = (main, side) if acc is None else (acc[0] + main, acc[1] + side)
    out_ref[:, :values] = acc[0].astype(jnp.bfloat16)
    out_ref[:, values:] = acc[1].astype(jnp.bfloat16)


def finish_kernel(heads, head_ref, ctx_ref, stats_ref, partial_ref, turn_ref, swap_ref, attention_ref, grad_ref, column):
    shards = partial_ref.shape[0]
    tokens = attention_ref.shape[0]
    values = attention_ref.shape[2]
    rows = stats_ref.shape[3]
    parts = [stats_ref[c, head_ref[0]] for c in range(shards)]
    parts = [(p[0:1], p[1:2], p[2:3]) for p in parts]
    top, shares, mass, delta = combine(parts)
    factors = [f / mass for f in shares]
    shifts = [p[2] - delta for p in parts]
    table = jnp.concatenate(factors + shifts + [jnp.zeros((128 - 2 * shards, rows), jnp.float32)], axis=0)
    column[...] = jnp.transpose(table)
    for t in range(tokens):
        start = pl.multiple_of((ctx_ref[0] * tokens + t) * heads, heads)
        own = column[pl.ds(start, heads), :]
        attended = jnp.zeros((heads, values), jnp.float32)
        rotated = jnp.zeros((heads, grad_ref.shape[2]), jnp.float32)
        for c in range(shards):
            factor = own[:, c : c + 1]
            shift = own[:, shards + c : shards + c + 1]
            first = partial_ref[c, t, :heads, :].astype(jnp.float32)
            second = partial_ref[c, t, heads:, :].astype(jnp.float32)
            attended = attended + factor * first[:, :values]
            rotated = rotated + factor * (second + shift * first)
        attention_ref[t] = attended.astype(jnp.bfloat16)
        rotated = rotated * softmax_scale
        grad_ref[t, :, :values] = rotated[:, :values]
        rope = rotated[:, values:]
        swapped = jnp.dot(rope, swap_ref[...], preferred_element_type=jnp.float32, precision=lax.Precision.HIGHEST)
        grad_ref[t, :, values:] = rope * turn_ref[t, 0:1, :] - swapped * turn_ref[t, 1:2, :]


def whole(space=pltpu.VMEM):
    return pl.BlockSpec(memory_space=space)


def body(query, cache, cotangent, positions, visible, *, shards, groups):
    tokens, heads, width = query.shape
    values = cotangent.shape[2]
    rotary = width - values
    keys = cache.shape[0]
    rows = shards * tokens * heads
    first_key = (lax.axis_index("ctx") * keys).astype(jnp.int32).reshape(1)
    ctx = lax.axis_index("ctx").astype(jnp.int32).reshape(1)
    head = lax.axis_index("head").astype(jnp.int32).reshape(1)
    cos_table, sin_table = rotation_tables(rotary // 2)
    swap = jnp.asarray(swap_matrix(rotary // 2))
    smem, vmem, hbm = whole(pltpu.SMEM), whole(), whole(pl.ANY)

    packed, turn = pl.pallas_call(
        prepare_kernel,
        out_shape=(
            jax.ShapeDtypeStruct((shards, tokens, heads, values + width), jnp.bfloat16),
            jax.ShapeDtypeStruct((tokens, 2, rotary), jnp.float32),
        ),
        in_specs=[smem] + [vmem] * 5,
        out_specs=(vmem, vmem),
        name="prepare",
    )(positions, query, cotangent, jnp.asarray(cos_table), jnp.asarray(sin_table), swap)
    packed = lax.all_to_all(packed, "ctx", 0, 0, tiled=True).reshape(rows, values + width)

    slots, offsets = [packed], [0]
    bit = groups // 2
    while bit:
        pairs = [(h, h ^ bit) for h in range(groups)]
        slots = slots + [lax.ppermute(s, "head", pairs) for s in slots]
        offsets = offsets + [o ^ bit for o in offsets]
        bit //= 2

    chunks = 8
    weights, stats = pl.pallas_call(
        functools.partial(score_kernel, chunks, heads),
        out_shape=(
            jax.ShapeDtypeStruct((shards * tokens, 2 * heads, keys), jnp.bfloat16),
            jax.ShapeDtypeStruct((shards * groups, 8, rows), jnp.float32),
        ),
        in_specs=[smem, smem, vmem, hbm],
        out_specs=(vmem, vmem),
        scratch_shapes=[
            pltpu.VMEM((keys, width), jnp.bfloat16),
            pltpu.VMEM((rows, keys), jnp.float32),
            pltpu.VMEM((rows, keys), jnp.float32),
            pltpu.SemaphoreType.DMA((chunks,)),
        ],
        name="score",
    )(first_key, visible, packed, cache)
    stats = lax.all_to_all(stats, ("ctx", "head"), 0, 0, tiled=True).reshape(shards, groups, 8, rows)

    partial = jnp.einsum("tak,kl->tal", weights, cache, preferred_element_type=jnp.float32).astype(jnp.bfloat16)
    partial = lax.all_to_all(partial, "ctx", 0, 0, tiled=True).reshape(shards, tokens, 2 * heads, width)

    size = 512
    total = rows * groups
    grad_cache = pl.pallas_call(
        functools.partial(latent_kernel, heads, tuple(offsets)),
        out_shape=jax.ShapeDtypeStruct((keys, width), jnp.bfloat16),
        grid=(keys // size,),
        in_specs=[smem, smem, smem, vmem, pl.BlockSpec((size, width), lambda i: (i, 0))] + [hbm] * groups,
        out_specs=pl.BlockSpec((size, width), lambda i: (i, 0)),
        scratch_shapes=[
            pltpu.VMEM((total, values + width), jnp.bfloat16),
            pltpu.VMEM((1, total), jnp.float32),
            pltpu.VMEM((1, total), jnp.float32),
            pltpu.VMEM((1, total), jnp.int32),
            pltpu.SemaphoreType.DMA((groups,)),
        ],
        name="latent",
    )(first_key, head, visible, stats, cache, *slots)

    attention, grad_query = pl.pallas_call(
        functools.partial(finish_kernel, heads),
        out_shape=(
            jax.ShapeDtypeStruct((tokens, heads, values), jnp.bfloat16),
            jax.ShapeDtypeStruct((tokens, heads, width), jnp.float32),
        ),
        in_specs=[smem, smem] + [vmem] * 4,
        out_specs=(vmem, vmem),
        scratch_shapes=[pltpu.VMEM((rows, 128), jnp.float32)],
        name="finish",
    )(head, ctx, stats, partial, turn, swap)
    return attention, grad_query, grad_cache


def solution(mesh):
    shards, groups = mesh.shape["ctx"], mesh.shape["head"]
    placed = (P("ctx", "head", None), P("ctx", None), P("ctx", "head", None), P("ctx"), P())
    return jax.shard_map(
        functools.partial(body, shards=shards, groups=groups),
        mesh=mesh,
        in_specs=placed,
        out_specs=(P("ctx", "head", None), P("ctx", "head", None), P("ctx", None)),
        check_vma=False,
    )
```

time: 340 us -> 84.5 us (0.25)
  blocking collectives: 285 us -> 0 us
  Pallas kernels: 0 us -> 28.5 us
  matrix products: 22.1 us -> 5.55 us
  starting transfers between devices: 0.08 us -> 15.8 us
  local copies, waits for them, and re-layouts: 2.48 us -> 17.5 us
  waiting for transfers between devices: 0.04 us -> 15 us
  other arithmetic: 14.8 us -> 0 us
  between operations: 15.2 us -> 1.33 us
    psum x3 -> x0, blocking collectives: 200 us -> none  [the longest x1 164 us: body(): grad_cache = lax.psum(grad_latent, 'head').astype(jnp.bfloat16)]
    all_gather x2 -> x0, blocking collectives: 63.1 us -> none  [the longest x1 32.5 us: body(): lax.all_gather(cotangent, 'ctx', axis=0, tiled=True)]
    pallas_call x0 -> x4, Pallas kernels: none -> 28.5 us  [the longest x1 16.6 us: body(): pl.pallas_call(functools.partial(latent_kernel, heads, tuple(offsets)), o...]
    pmax x1 -> x0, blocking collectives: 21.4 us -> none  [body(): peak = lax.pmax(local_peak, 'ctx')]
    dot_general x6 -> x1, matrix products: 22.1 us -> 5.55 us  [body(): jnp.einsum('tak,kl->tal', weights, cache, preferred_element_type=jnp.floa...]
    unnamed x8 -> x12, local copies, waits for them, and re-layouts: 1 us -> 17.5 us
    all_to_all x0 -> x3, waiting for transfers between devices: none -> 15 us  [the longest x1 10.3 us: body(): lax.all_to_all(partial, 'ctx', 0, 0, tiled=True)]
    all_to_all x0 -> x3, starting transfers between devices: none -> 13.8 us  [the longest x1 7.31 us: body(): lax.all_to_all(packed, 'ctx', 0, 0, tiled=True)]
  transfers between devices with their start and end apart: 2 -> 6, of which waited for: 0 -> 3; matrix products, arithmetic and copies ran while one was open for 4% -> 16% of each run, Pallas kernels for 0% -> 12%
where the time goes in v1:
time: 84.5 us; the launch traced here: 83.7 us
  Pallas kernels  28.5 us (34%)
  local copies, waits for them, and re-layouts  17.5 us (21%)
  starting transfers between devices  15.8 us (19%)
  waiting for transfers between devices  15 us (18%)
  matrix products  5.55 us (7%)
  between operations  1.33 us (2%)
    unnamed x12, local copies, waits for them, and re-layouts  17.5 us
    pallas_call x1, Pallas kernels, body(): pl.pallas_call(functools.partial(latent_kernel, heads, tuple(offsets)), o...  16.6 us
    all_to_all x1, waiting for transfers between devices, body(): lax.all_to_all(partial, 'ctx', 0, 0, tiled=True)  10.3 us
    pallas_call x1, Pallas kernels, body(): pl.pallas_call(functools.partial(score_kernel, chunks, heads), out_shape=...  8.19 us
    all_to_all x1, starting transfers between devices, body(): lax.all_to_all(packed, 'ctx', 0, 0, tiled=True)  7.31 us
    dot_general x1, matrix products, body(): jnp.einsum('tak,kl->tal', weights, cache, preferred_element_type=jnp.floa...  5.55 us
    all_to_all x1, starting transfers between devices, body(): lax.all_to_all(partial, 'ctx', 0, 0, tiled=True)  3.43 us
    all_to_all x1, starting transfers between devices, body(): lax.all_to_all(stats, ('ctx', 'head'), 0, 0, tiled=True)  3.04 us
  transfers between devices with their start and end apart: 6, of which 3 were waited for; matrix products, arithmetic and copies ran while one was open for 16% of the time, Pallas kernels for 12%

profile of v1, /device:TPU:0, one launch (start us, length us, event | category | flops | bytes accessed | tf_op | source)
XLA Modules:
  0.0 83.7 jit_solution(12005507433272673459)
XLA Ops:
  1.3 1.7 %prepare.1 = (bf16[8,1,16,1088]{3,2,1,0:T(8,128)(2,1)}, f32[1,2,64]{2,1,0:T(2,128)}) custom-call(s32[1]{0:T(128)S(6)} %copy.14.position_ref, bf16[1,16,576]{2,1,0:T(8,128)(2,1)} %query_ref.1, bf16[1,16,512]{2,1,0:T(8,128)(2,1)} %cotangent_ref.1, f32[18,64]{1,0:T(8,128)} %constant.18.clone.cos_ref, f32[18,64]{1,0:T(8,128)} %constant.19.clone.sin_ref, ...), custom_call_target="tpu_custom_call" | custom-call | tf_op jit(solution)/shard_map/prepare/pallas_call | solution.py:229
  3.0 7.3 %all-to-all-start = ((bf16[8,1,16,1088]{3,2,1,0:T(8,128)(2,1)}), bf16[8,1,16,1088]{3,2,1,0:T(8,128)(2,1)}, u32[]{:S(2)}, u32[]{:S(2)}) async-start(bf16[8,1,16,1088]{3,2,1,0:T(8,128)(2,1)} %get-tuple-element.9), calls=%async_computation | async-start | bytes 589824 | tf_op jit(solution)/shard_map/all_to_all | solution.py:239
  10.3 7.7 %copy.11.cache_ref = bf16[4096,576]{1,0:T(8,128)(2,1)} copy(bf16[4096,576]{0,1:T(8,128)(2,1)} %param.9) | data formatting | bytes 9437184 | tf_op args[1]
  17.9 2.0 %all-to-all-done = bf16[8,1,16,1088]{3,2,1,0:T(8,128)(2,1)} async-done(((bf16[8,1,16,1088]{3,2,1,0:T(8,128)(2,1)}), bf16[8,1,16,1088]{3,2,1,0:T(8,128)(2,1)}, u32[]{:S(2)}, u32[]{:S(2)}) %all-to-all-start) | async-done | bytes 278560 | tf_op jit(solution)/shard_map/all_to_all | solution.py:239
  20.0 1.5 %collective-permute-start = (bf16[128,1088]{1,0:T(8,128)(2,1)}, bf16[128,1088]{1,0:T(8,128)(2,1)S(1)}, u32[]{:S(2)}, u32[]{:S(2)}) collective-permute-start(bf16[128,1088]{1,0:T(8,128)(2,1)} %bitcast.3.packed_ref.refs_0_), channel_id=1, source_target_pairs={{0,2},{1,3},{2,0},{3,1},{4,6},{5,7},{6,4},{7,5},{8,10},{9,11},{10,... | collective-permute-start | bytes 835592 | tf_op jit(solution)/shard_map/ppermute | solution.py:245
  21.5 8.2 %score.1 = (bf16[8,32,4096]{2,1,0:T(8,128)(2,1)}, f32[32,8,128]{2,1,0:T(8,128)}) custom-call(s32[1]{0:T(128)} %bitcast.2.first_ref, s32[8]{0:T(128)} %visible_ref.3, bf16[128,1088]{1,0:T(8,128)(2,1)} %bitcast.3.packed_ref.refs_0_, bf16[4096,576]{1,0:T(8,128)(2,1)} %copy.11.cache_ref), custom_call_target="tpu_custom_call" | custom-call | tf_op jit(solution)/shard_map/score/pallas_call | solution.py:250
  29.7 3.0 %all-to-all-start.1 = ((f32[32,8,128]{2,1,0:T(8,128)}), f32[32,8,128]{2,1,0:T(8,128)S(1)}, u32[]{:S(2)}, u32[]{:S(2)}) async-start(f32[32,8,128]{2,1,0:T(8,128)} %get-tuple-element.10), calls=%async_computation.1 | async-start | bytes 262144 | tf_op jit(solution)/shard_map/all_to_all | solution.py:266
  32.7 5.5 %fusion.2 = bf16[8,32,576]{2,1,0:T(8,128)(2,1)} fusion(bf16[8,32,4096]{2,1,0:T(8,128)(2,1)} %get-tuple-element.11, bf16[4096,576]{0,1:T(8,128)(2,1)} %param.9), kind=kOutput, calls=%fused_computation.2 | convolution fusion | flops 1208107008 | bytes 7110656 | tf_op jit(solution)/shard_map/tak,kl->tal/dot_general | solution.py:268
  38.3 2.7 %all-to-all-done.1 = f32[32,8,128]{2,1,0:T(8,128)S(1)} async-done(((f32[32,8,128]{2,1,0:T(8,128)}), f32[32,8,128]{2,1,0:T(8,128)S(1)}, u32[]{:S(2)}, u32[]{:S(2)}) %all-to-all-start.1) | async-done | bytes 131104 | tf_op jit(solution)/shard_map/all_to_all | solution.py:266
  40.9 0.0 copy-start.1
  40.9 3.4 %all-to-all-start.2 = ((bf16[8,32,576]{2,1,0:T(8,128)(2,1)}), bf16[8,32,576]{2,1,0:T(8,128)(2,1)S(1)}, u32[]{:S(2)}, u32[]{:S(2)}) async-start(bf16[8,32,576]{2,1,0:T(8,128)(2,1)} %fusion.2), calls=%async_computation.2 | async-start | bytes 655360 | tf_op jit(solution)/shard_map/all_to_all | solution.py:269
  44.4 0.3 collective-permute-start.1
  44.6 0.0 collective-permute-done.refs_1_
  44.6 0.0 copy-start.2
  44.6 0.3 collective-permute-start.2
  44.9 10.3 %all-to-all-done.2 = bf16[8,32,576]{2,1,0:T(8,128)(2,1)S(1)} async-done(((bf16[8,32,576]{2,1,0:T(8,128)(2,1)}), bf16[8,32,576]{2,1,0:T(8,128)(2,1)S(1)}, u32[]{:S(2)}, u32[]{:S(2)}) %all-to-all-start.2) | async-done | bytes 294944 | tf_op jit(solution)/shard_map/all_to_all | solution.py:269
  55.2 0.0 copy-start
  55.2 0.0 copy-done.1
  55.2 0.7 copy-done
  55.9 2.1 %finish.1 = (bf16[1,16,512]{2,1,0:T(8,128)(2,1)}, f32[1,16,576]{2,1,0:T(8,128)}) custom-call(s32[1]{0:T(128)} %bitcast.head_ref, s32[1]{0:T(128)} %bitcast.1.ctx_ref, f32[8,4,8,128]{3,2,1,0:T(8,128)} %bitcast.13, bf16[8,1,32,576]{3,2,1,0:T(8,128)(2,1)} %bitcast.12, f32[1,2,64]{2,1,0:T(2,128)} %get-tuple-element.12.turn_ref, f32[64,64]{1,0:T(8,128)} %constant.17.clone.swap_ref), custom_call_target="tpu_custom_call" | custom-call | tf_op jit(solution)/shard_map/finish/pallas_call | solution.py:289
  58.0 0.0 collective-permute-done.1.refs_2_
  58.0 0.0 copy-start.3
  58.0 0.0 collective-permute-done.2.refs_3_
  58.0 0.0 copy-done.2
  58.0 0.7 copy-done.3
  58.7 0.0 copy-start.4
  58.7 0.7 copy-done.4
  59.4 16.6 %latent.1 = bf16[4096,576]{1,0:T(8,128)(2,1)} custom-call(s32[1]{0:T(128)} %bitcast.2.first_ref, s32[1]{0:T(128)} %bitcast.head_ref, s32[8]{0:T(128)} %visible_ref.3, f32[8,4,8,128]{3,2,1,0:T(8,128)} %bitcast.14, bf16[4096,576]{1,0:T(8,128)(2,1)} %copy.11.cache_ref, bf16[128,1088]{1,0:T(8,128)(2,1)} %bitcast.3.packed_ref.refs_0_, ...), custom_call_target="tpu_custom_call" | custom-call | tf_op jit(solution)/shard_map/latent/pallas_call | solution.py:273
  76.0 7.7 %copy.13 = bf16[4096,576]{0,1:T(8,128)(2,1)} copy(bf16[4096,576]{1,0:T(8,128)(2,1)} %latent.1) | data formatting | bytes 9437184
Async XLA Ops:
  3.0 17.0 %all-to-all-start = ((bf16[8,1,16,1088]{3,2,1,0:T(8,128)(2,1)}), bf16[8,1,16,1088]{3,2,1,0:T(8,128)(2,1)}, u32[]{:S(2)}, u32[]{:S(2)}) async-start(bf16[8,1,16,1088]{3,2,1,0:T(8,128)(2,1)} %get-tuple-element.9), calls=%async_computation | async-start | bytes 589824 | tf_op jit(solution)/shard_map/all_to_all | solution.py:239
  20.0 24.7 %collective-permute-start = (bf16[128,1088]{1,0:T(8,128)(2,1)}, bf16[128,1088]{1,0:T(8,128)(2,1)S(1)}, u32[]{:S(2)}, u32[]{:S(2)}) collective-permute-start(bf16[128,1088]{1,0:T(8,128)(2,1)} %bitcast.3.packed_ref.refs_0_), channel_id=1, source_target_pairs={{0,2},{1,3},{2,0},{3,1},{4,6},{5,7},{6,4},{7,5},{8,10},{9,11},{10,... | collective-permute-start | bytes 835592 | tf_op jit(solution)/shard_map/ppermute | solution.py:245
  29.7 11.2 %all-to-all-start.1 = ((f32[32,8,128]{2,1,0:T(8,128)}), f32[32,8,128]{2,1,0:T(8,128)S(1)}, u32[]{:S(2)}, u32[]{:S(2)}) async-start(f32[32,8,128]{2,1,0:T(8,128)} %get-tuple-element.10), calls=%async_computation.1 | async-start | bytes 262144 | tf_op jit(solution)/shard_map/all_to_all | solution.py:266
  40.9 14.3 %copy-start.1 = (f32[32,8,128]{2,1,0:T(8,128)}, f32[32,8,128]{2,1,0:T(8,128)S(1)}, u32[]{:S(2)}) copy-start(f32[32,8,128]{2,1,0:T(8,128)S(1)} %all-to-all-done.1) | copy-start | bytes 393220
  40.9 14.3 %all-to-all-start.2 = ((bf16[8,32,576]{2,1,0:T(8,128)(2,1)}), bf16[8,32,576]{2,1,0:T(8,128)(2,1)S(1)}, u32[]{:S(2)}, u32[]{:S(2)}) async-start(bf16[8,32,576]{2,1,0:T(8,128)(2,1)} %fusion.2), calls=%async_computation.2 | async-start | bytes 655360 | tf_op jit(solution)/shard_map/all_to_all | solution.py:269
  44.4 13.7 %collective-permute-start.1 = (bf16[128,1088]{1,0:T(8,128)(2,1)}, bf16[128,1088]{1,0:T(8,128)(2,1)S(1)}, u32[]{:S(2)}, u32[]{:S(2)}) collective-permute-start(bf16[128,1088]{1,0:T(8,128)(2,1)} %bitcast.3.packed_ref.refs_0_), channel_id=1, source_target_pairs={{0,1},{1,0},{2,3},{3,2},{4,5},{5,4},{6,7},{7,6},{8,9},{9,8},{10,11... | collective-permute-start | bytes 835592 | tf_op jit(solution)/shard_map/ppermute | solution.py:245
  44.6 13.4 %copy-start.2 = (bf16[128,1088]{1,0:T(8,128)(2,1)}, bf16[128,1088]{1,0:T(8,128)(2,1)S(1)}, u32[]{:S(2)}) copy-start(bf16[128,1088]{1,0:T(8,128)(2,1)S(1)} %collective-permute-done.refs_1_) | copy-start | bytes 835588
  44.6 13.4 %collective-permute-start.2 = (bf16[128,1088]{1,0:T(8,128)(2,1)S(1)}, bf16[128,1088]{1,0:T(8,128)(2,1)S(1)}, u32[]{:S(2)}, u32[]{:S(2)}) collective-permute-start(bf16[128,1088]{1,0:T(8,128)(2,1)S(1)} %collective-permute-done.refs_1_), channel_id=1, source_target_pairs={{0,1},{1,0},{2,3},{3,2},{4,5},{5,4},{6,7},{7,6},{8,9},{9,8},{10,11... | collective-permute-start | bytes 835592 | tf_op jit(solution)/shard_map/ppermute | solution.py:245
  55.2 0.7 copy-start
  58.0 0.7 copy-start.3
  58.7 0.7 copy-start.4
